TPU v7x, 256 devices: a whole 4x4x8 slice. The times are simulated.
256 devices in a mesh: samp: 4 (over y), snp: 64 (over x, z, core).
Axes of the slice: x: 4, y: 4, z: 8, core: 2. Of those that a mesh axis runs over, the one named last changes fastest.
Arguments:
- dosage: bfloat16 [8192, 32768], P('samp', 'snp'), may hold values from 0 to 2
- band_width: int32 [64], P('snp'), may hold values from 1 to 3, as said below
- marginal: float32 [32768, 64], P('snp'), may hold values from -6 to 6
- penalty: float32 [64], replicated, may hold values from 4 to 16
Outputs:
- effects: float32 [32768, 64], P('snp')
- residual: float32 [32768, 64], P('snp')
Inputs may be any that keep to these rules, and one draw needn't show every extreme that they name: `band_width`: every draw has a block with 3 neighbours and one with a single neighbour.
All inputs are finite; a program needn't handle non-finite values.
Results may differ from a plain program's by a relative error of at most 0.00087.
Values may be sent and summed in bfloat16 or wider, within the bound.
A program may use at most 64 MiB of HBM per device.

v0:
```python
import jax
import jax.numpy as jnp
from jax import lax
from jax.sharding import PartitionSpec as P

WMAX = 3
ITERS = 2


def sent_to_all(shard, axis):
    copies = jnp.broadcast_to(shard, (lax.axis_size(axis), *shard.shape))
    return lax.all_to_all(copies, axis, split_axis=0, concat_axis=0, tiled=True)


def of_everyone(shard, axis):
    return sent_to_all(shard, axis).sum(axis=0)


def from_behind(block, axis, distance):
    devices = range(lax.axis_size(axis))
    route = [(i - distance, i) for i in devices if i - distance in devices]
    return lax.ppermute(block, axis, route)


def in_one(arrays, axis):
    ends = [0]
    for a in arrays:
        ends.append(ends[-1] + a.size)
    subtotal = of_everyone(jnp.concatenate([a.ravel() for a in arrays]), axis)
    return tuple((subtotal[b:e].reshape(a.shape) for a, b, e in zip(arrays, ends, ends[1:])))


def cut_along(shard, dim, devices):
    lengths = shard.shape
    parts = shard.reshape(*lengths[:dim], devices, lengths[dim] // devices, *lengths[dim + 1 :])
    return jnp.moveaxis(parts, dim, 0)


def summed_on_arrival(shard, axis, dim):
    parts = cut_along(shard, dim, lax.axis_size(axis))
    arrived = lax.all_to_all(parts, axis, split_axis=0, concat_axis=0, tiled=True)
    return arrived.sum(axis=0)


def gram_pair(scaled, other):
    return lax.dot_general(
        scaled, other, (((0,), (0,)), ((), ())), preferred_element_type=jnp.float32
    )


def exact_dot(left_mat, right_mat):
    return jnp.dot(left_mat, right_mat, precision=lax.Precision.HIGHEST)


def exact_tdot(left_mat, right_mat):
    return lax.dot_general(
        left_mat, right_mat, (((0,), (0,)), ((), ())), precision=lax.Precision.HIGHEST
    )


def residual_sum(vector):
    return of_everyone(jnp.sum(vector * vector, 0), "snp")


def search_sum(direction, imaged):
    return of_everyone(jnp.sum(direction * imaged, 0), "snp")


def fetch_ahead(values, position, sections):
    for section in range(sections):
        moved = from_behind(values, "snp", -(1 << section))
        values = jnp.where((position >> section) % 2 == 1, moved, values)
    return values


def send_ahead(values, position, sections):
    for section in range(sections):
        moved = from_behind(values, "snp", 1 << section)
        values = jnp.where((position >> section) % 2 == 1, moved, values)
    return values


def shards(dosage, band_width, marginal, penalty):
    samples = dosage.shape[0] * lax.axis_size("samp")
    genotype = dosage.astype(jnp.float32)
    col_sum, col_sq = in_one((jnp.sum(genotype, 0), jnp.sum(genotype * genotype, 0)), "samp")
    center = col_sum / samples
    spread = col_sq / samples - center * center
    scaled = ((genotype - center) * lax.rsqrt(spread + 1e-05)).astype(jnp.bfloat16)
    own_width = band_width[0]
    pieces = [gram_pair(scaled, scaled)]
    for offset in range(1, WMAX + 1):
        ahead_cols = from_behind(scaled, "snp", -offset)
        gram_piece = jnp.where(offset <= own_width, gram_pair(scaled, ahead_cols), 0.0)
        pieces.append(gram_piece)
    partial_band = jnp.concatenate(pieces, 1)
    ld_piece = summed_on_arrival(partial_band, "samp", 1) / samples
    position = lax.axis_index("samp")
    sections = WMAX.bit_length()
    effects = jnp.zeros_like(marginal)
    residual = marginal
    direction = marginal
    norm_now = residual_sum(residual)
    for sweep in range(ITERS):
        chosen = fetch_ahead(direction, position, sections)
        result = exact_dot(ld_piece, chosen)
        backward = jnp.where(position > 0, exact_tdot(ld_piece, direction), 0.0)
        result = result + send_ahead(backward, position, sections)
        imaged = of_everyone(result, "samp") + penalty * direction
        step_size = norm_now / search_sum(direction, imaged)
        effects = effects + step_size * direction
        residual = residual - step_size * imaged
        norm_next = residual_sum(residual)
        direction = residual + norm_next / norm_now * direction
        norm_now = norm_next
    return (effects, residual)


def solution(mesh):
    in_specs = (P("samp", "snp"), P("snp"), P("snp", None), P())
    out_specs = (P("snp", None), P("snp", None))
    return jax.shard_map(shards, mesh=mesh, in_specs=in_specs, out_specs=out_specs, check_vma=False)
```

profile of v0, /device:TPU:1, one launch (start us, length us, event | category | flops | bytes accessed | tf_op | source)
XLA Modules:
  0.0 341.6 jit_solution(6114165446057236473)
XLA Ops:
  0.6 2.3 convert_reduce_fusion
  3.0 9.0 %all_to_all.45 = f32[4,1,1024]{2,1,0:T(1,128)S(1)} all-to-all(f32[4,1,1024]{2,1,0:T(1,128)S(1)} %broadcast_in_dim.42), channel_id=1, replica_groups=mesh['samp'=4,'snp'=64] {'samp'}, dimensions={0} | all-to-all | bytes 32768 | tf_op jit(solution)/shard_map/all_to_all | solution.py:12
  12.1 0.5 fusion.2
  12.6 1.3 collective-permute-start.2
  13.9 1.3 collective-permute-start.1
  15.2 4.0 %collective-permute-start = (bf16[2048,512]{1,0:T(8,128)(2,1)S(1)}, bf16[2048,512]{1,0:T(8,128)(2,1)S(1)}, u32[]{:S(2)}, u32[]{:S(2)}) collective-permute-start(bf16[2048,512]{1,0:T(8,128)(2,1)S(1)} %fusion.2), channel_id=1, source_target_pairs={{1,0},{2,1},{3,2},{4,3},{5,4},{6,5},{7,6},{8,7},{9,8},{10,9},{11,1... | collective-permute-start | bytes 6291464 | tf_op jit(solution)/shard_map/ppermute | solution.py:22
  19.9 1.3 fusion.19
  21.2 67.0 %collective-permute-done.2 = bf16[2048,512]{1,0:T(8,128)(2,1)S(1)} collective-permute-done((bf16[2048,512]{1,0:T(8,128)(2,1)S(1)}, bf16[2048,512]{1,0:T(8,128)(2,1)S(1)}, u32[]{:S(2)}, u32[]{:S(2)}) %collective-permute-start.2) | collective-permute-done | bytes 2097184 | tf_op jit(solution)/shard_map/ppermute | solution.py:22
  88.1 1.3 convolution_select_fusion
  89.4 40.0 %collective-permute-done.1 = bf16[2048,512]{1,0:T(8,128)(2,1)S(1)} collective-permute-done((bf16[2048,512]{1,0:T(8,128)(2,1)S(1)}, bf16[2048,512]{1,0:T(8,128)(2,1)S(1)}, u32[]{:S(2)}, u32[]{:S(2)}) %collective-permute-start.1) | collective-permute-done | bytes 2097184 | tf_op jit(solution)/shard_map/ppermute | solution.py:22
  129.4 1.3 convolution_select_fusion.1
  130.7 0.6 collective-permute-done
  131.3 1.3 convolution_select_fusion.2
  132.6 2.4 pad_maximum_fusion
  135.0 5.0 %all-to-all-start.2 = ((f32[4,512,512]{1,2,0:T(8,128)}), f32[4,512,512]{1,2,0:T(8,128)}, u32[]{:S(2)}, u32[]{:S(2)}) async-start(f32[4,512,512]{1,2,0:T(8,128)} %bitcast.20), calls=%async_computation.2 | async-start | bytes 8388608 | tf_op jit(solution)/shard_map/all_to_all | solution.py:41
  140.0 1.9 collective-permute-start.3
  141.9 24.7 %all-to-all-done.2 = f32[4,512,512]{1,2,0:T(8,128)} async-done(((f32[4,512,512]{1,2,0:T(8,128)}), f32[4,512,512]{1,2,0:T(8,128)}, u32[]{:S(2)}, u32[]{:S(2)}) %all-to-all-start.2) | async-done | bytes 4194336 | tf_op jit(solution)/shard_map/all_to_all | solution.py:41
  166.6 2.8 reduce_sum.131
  169.4 1.2 convolution_select_fusion.4
  170.6 8.6 %collective-permute-start.5 = (f32[512,64]{0,1:T(8,128)S(1)}, f32[512,64]{0,1:T(8,128)S(1)}, u32[]{:S(2)}, u32[]{:S(2)}) collective-permute-start(f32[512,64]{0,1:T(8,128)S(1)} %convolution_select_fusion.4), channel_id=1, source_target_pairs={{0,1},{1,2},{2,3},{3,4},{4,5},{5,6},{6,7},{7,8},{8,9},{9,10},{10,1... | collective-permute-start | bytes 393224 | tf_op jit(solution)/shard_map/ppermute | solution.py:22
  179.3 1.3 collective-permute-start.4
  180.6 0.6 collective-permute-done.5
  181.2 41.6 %collective-permute-start.6 = (f32[512,64]{0,1:T(8,128)S(1)}, f32[512,64]{0,1:T(8,128)S(1)}, u32[]{:S(2)}, u32[]{:S(2)}) collective-permute-start(f32[512,64]{0,1:T(8,128)S(1)} %broadcast_select_fusion.2), channel_id=1, source_target_pairs={{0,2},{1,3},{2,4},{3,5},{4,6},{5,7},{6,8},{7,9},{8,10},{9,11},{10,... | collective-permute-start | bytes 393224 | tf_op jit(solution)/shard_map/ppermute | solution.py:22
  222.8 0.3 collective-permute-done.4
  223.1 1.6 collective-permute-done.6
  224.7 0.8 convolution_add_fusion.1
  225.5 0.1 broadcast_in_dim.45
  225.5 9.3 %all_to_all.46 = f32[4,512,64]{1,2,0:T(8,128)S(1)} all-to-all(f32[4,512,64]{1,2,0:T(8,128)S(1)} %broadcast_in_dim.45), channel_id=1, replica_groups=mesh['samp'=4,'snp'=64] {'samp'}, dimensions={0} | all-to-all | bytes 1048576 | tf_op jit(solution)/shard_map/all_to_all | solution.py:12
  234.9 0.2 multiply_reduce_fusion.2
  235.1 27.0 %all_to_all.47 = f32[64,1,64]{2,1,0:T(1,128)S(1)} all-to-all(f32[64,1,64]{2,1,0:T(1,128)S(1)} %broadcast_in_dim.41), channel_id=1, replica_groups=mesh['samp'=4,'snp'=64] {'snp'}, dimensions={0} | all-to-all | bytes 32768 | tf_op jit(solution)/shard_map/all_to_all | solution.py:12
  262.1 0.6 broadcast_in_dim.46
  262.8 4.9 %all-to-all-start.4 = ((f32[64,1,64]{2,1,0:T(1,128)}), f32[64,1,64]{2,1,0:T(1,128)S(1)}, u32[]{:S(2)}, u32[]{:S(2)}) async-start(f32[64,1,64]{2,1,0:T(1,128)} %broadcast_in_dim.46), calls=%async_computation.4 | async-start | bytes 65536 | tf_op jit(solution)/shard_map/all_to_all | solution.py:12
  267.7 9.3 %all-to-all-done.4 = f32[64,1,64]{2,1,0:T(1,128)S(1)} async-done(((f32[64,1,64]{2,1,0:T(1,128)}), f32[64,1,64]{2,1,0:T(1,128)S(1)}, u32[]{:S(2)}, u32[]{:S(2)}) %all-to-all-start.4) | async-done | bytes 16416 | tf_op jit(solution)/shard_map/all_to_all | solution.py:12
  277.0 0.2 multiply_reduce_fusion.1
  277.3 13.3 %all_to_all.48 = f32[64,1,64]{2,1,0:T(1,128)S(1)} all-to-all(f32[64,1,64]{2,1,0:T(1,128)S(1)} %broadcast_in_dim.47), channel_id=1, replica_groups=mesh['samp'=4,'snp'=64] {'snp'}, dimensions={0} | all-to-all | bytes 32768 | tf_op jit(solution)/shard_map/all_to_all | solution.py:12
  290.6 0.1 multiply_add_fusion.2
  290.7 1.2 convolution_select_fusion.3
  291.9 2.8 collective-permute-start.9
  294.7 1.9 collective-permute-start.7
  296.7 2.3 collective-permute-start.10
  298.9 2.1 collective-permute-done.7
  301.0 1.3 collective-permute-start.8
  302.3 5.2 %collective-permute-done.8 = f32[512,64]{0,1:T(8,128)S(1)} collective-permute-done((f32[512,64]{0,1:T(8,128)S(1)}, f32[512,64]{0,1:T(8,128)S(1)}, u32[]{:S(2)}, u32[]{:S(2)}) %collective-permute-start.8) | collective-permute-done | bytes 131104 | tf_op jit(solution)/shard_map/ppermute | solution.py:22
  307.5 0.8 convolution_add_fusion
  308.4 10.4 %all_to_all.49 = f32[4,512,64]{1,2,0:T(8,128)S(1)} all-to-all(f32[4,512,64]{1,2,0:T(8,128)S(1)} %broadcast_in_dim.48), channel_id=1, replica_groups=mesh['samp'=4,'snp'=64] {'samp'}, dimensions={0} | all-to-all | bytes 1048576 | tf_op jit(solution)/shard_map/all_to_all | solution.py:12
  318.8 0.2 multiply_reduce_fusion
  319.1 21.6 %all_to_all.50 = f32[64,1,64]{2,1,0:T(1,128)S(1)} all-to-all(f32[64,1,64]{2,1,0:T(1,128)S(1)} %broadcast_in_dim.49), channel_id=1, replica_groups=mesh['samp'=4,'snp'=64] {'snp'}, dimensions={0} | all-to-all | bytes 32768 | tf_op jit(solution)/shard_map/all_to_all | solution.py:12
  340.7 0.8 multiply_subtract_fusion
  (30 shorter events, 0.5 us)
Async XLA Ops:
  0.6 11.4 %copy-start = (bf16[2048,512]{1,0:T(8,128)(2,1)S(1)}, bf16[2048,512]{1,0:T(8,128)(2,1)}, u32[]{:S(2)}) copy-start(bf16[2048,512]{1,0:T(8,128)(2,1)} %param.4) | copy-start | bytes 6291460
  12.6 75.5 %collective-permute-start.2 = (bf16[2048,512]{1,0:T(8,128)(2,1)S(1)}, bf16[2048,512]{1,0:T(8,128)(2,1)S(1)}, u32[]{:S(2)}, u32[]{:S(2)}) collective-permute-start(bf16[2048,512]{1,0:T(8,128)(2,1)S(1)} %fusion.2), channel_id=1, source_target_pairs={{3,0},{4,1},{5,2},{6,3},{7,4},{8,5},{9,6},{10,7},{11,8},{12,9},{13... | collective-permute-start | bytes 6291464 | tf_op jit(solution)/shard_map/ppermute | solution.py:22
  13.9 115.5 %collective-permute-start.1 = (bf16[2048,512]{1,0:T(8,128)(2,1)S(1)}, bf16[2048,512]{1,0:T(8,128)(2,1)S(1)}, u32[]{:S(2)}, u32[]{:S(2)}) collective-permute-start(bf16[2048,512]{1,0:T(8,128)(2,1)S(1)} %fusion.2), channel_id=1, source_target_pairs={{2,0},{3,1},{4,2},{5,3},{6,4},{7,5},{8,6},{9,7},{10,8},{11,9},{12,... | collective-permute-start | bytes 6291464 | tf_op jit(solution)/shard_map/ppermute | solution.py:22
  15.2 116.1 %collective-permute-start = (bf16[2048,512]{1,0:T(8,128)(2,1)S(1)}, bf16[2048,512]{1,0:T(8,128)(2,1)S(1)}, u32[]{:S(2)}, u32[]{:S(2)}) collective-permute-start(bf16[2048,512]{1,0:T(8,128)(2,1)S(1)} %fusion.2), channel_id=1, source_target_pairs={{1,0},{2,1},{3,2},{4,3},{5,4},{6,5},{7,6},{8,7},{9,8},{10,9},{11,1... | collective-permute-start | bytes 6291464 | tf_op jit(solution)/shard_map/ppermute | solution.py:22
  135.0 5.0 %copy-start.1 = (f32[512,64]{0,1:T(8,128)S(1)}, f32[512,64]{0,1:T(8,128)}, u32[]{:S(2)}) copy-start(f32[512,64]{0,1:T(8,128)} %param.6) | copy-start | bytes 393220
  135.0 31.7 %all-to-all-start.2 = ((f32[4,512,512]{1,2,0:T(8,128)}), f32[4,512,512]{1,2,0:T(8,128)}, u32[]{:S(2)}, u32[]{:S(2)}) async-start(f32[4,512,512]{1,2,0:T(8,128)} %bitcast.20), calls=%async_computation.2 | async-start | bytes 8388608 | tf_op jit(solution)/shard_map/all_to_all | solution.py:41
  140.0 39.2 %collective-permute-start.3 = (f32[512,64]{0,1:T(8,128)S(1)}, f32[512,64]{0,1:T(8,128)S(1)}, u32[]{:S(2)}, u32[]{:S(2)}) collective-permute-start(f32[512,64]{0,1:T(8,128)S(1)} %copy-done.1), channel_id=1, source_target_pairs={{1,0},{2,1},{3,2},{4,3},{5,4},{6,5},{7,6},{8,7},{9,8},{10,9},{11,1... | collective-permute-start | bytes 393224 | tf_op jit(solution)/shard_map/ppermute | solution.py:22
  170.6 10.6 %collective-permute-start.5 = (f32[512,64]{0,1:T(8,128)S(1)}, f32[512,64]{0,1:T(8,128)S(1)}, u32[]{:S(2)}, u32[]{:S(2)}) collective-permute-start(f32[512,64]{0,1:T(8,128)S(1)} %convolution_select_fusion.4), channel_id=1, source_target_pairs={{0,1},{1,2},{2,3},{3,4},{4,5},{5,6},{6,7},{7,8},{8,9},{9,10},{10,1... | collective-permute-start | bytes 393224 | tf_op jit(solution)/shard_map/ppermute | solution.py:22
  179.3 43.9 %collective-permute-start.4 = (f32[512,64]{0,1:T(8,128)S(1)}, f32[512,64]{0,1:T(8,128)S(1)}, u32[]{:S(2)}, u32[]{:S(2)}) collective-permute-start(f32[512,64]{0,1:T(8,128)S(1)} %broadcast_select_fusion.3), channel_id=1, source_target_pairs={{2,0},{3,1},{4,2},{5,3},{6,4},{7,5},{8,6},{9,7},{10,8},{11,9},{12,... | collective-permute-start | bytes 393224 | tf_op jit(solution)/shard_map/ppermute | solution.py:22
  181.2 53.8 %copy-start.2 = (f32[64]{0:T(128)S(1)}, f32[64]{0:T(128)}, u32[]{:S(2)}) copy-start(f32[64]{0:T(128)} %param.7) | copy-start | bytes 772
  181.2 43.5 %collective-permute-start.6 = (f32[512,64]{0,1:T(8,128)S(1)}, f32[512,64]{0,1:T(8,128)S(1)}, u32[]{:S(2)}, u32[]{:S(2)}) collective-permute-start(f32[512,64]{0,1:T(8,128)S(1)} %broadcast_select_fusion.2), channel_id=1, source_target_pairs={{0,2},{1,3},{2,4},{3,5},{4,6},{5,7},{6,8},{7,9},{8,10},{9,11},{10,... | collective-permute-start | bytes 393224 | tf_op jit(solution)/shard_map/ppermute | solution.py:22
  262.8 14.2 %all-to-all-start.4 = ((f32[64,1,64]{2,1,0:T(1,128)}), f32[64,1,64]{2,1,0:T(1,128)S(1)}, u32[]{:S(2)}, u32[]{:S(2)}) async-start(f32[64,1,64]{2,1,0:T(1,128)} %broadcast_in_dim.46), calls=%async_computation.4 | async-start | bytes 65536 | tf_op jit(solution)/shard_map/all_to_all | solution.py:12
  291.9 4.7 %collective-permute-start.9 = (f32[512,64]{0,1:T(8,128)S(1)}, f32[512,64]{0,1:T(8,128)S(1)}, u32[]{:S(2)}, u32[]{:S(2)}) collective-permute-start(f32[512,64]{0,1:T(8,128)S(1)} %convolution_select_fusion.3), channel_id=1, source_target_pairs={{0,1},{1,2},{2,3},{3,4},{4,5},{5,6},{6,7},{7,8},{8,9},{9,10},{10,1... | collective-permute-start | bytes 393224 | tf_op jit(solution)/shard_map/ppermute | solution.py:22
  294.7 6.3 %collective-permute-start.7 = (f32[512,64]{0,1:T(8,128)S(1)}, f32[512,64]{0,1:T(8,128)S(1)}, u32[]{:S(2)}, u32[]{:S(2)}) collective-permute-start(f32[512,64]{0,1:T(8,128)S(1)} %multiply_add_fusion.2), channel_id=1, source_target_pairs={{1,0},{2,1},{3,2},{4,3},{5,4},{6,5},{7,6},{8,7},{9,8},{10,9},{11,1... | collective-permute-start | bytes 393224 | tf_op jit(solution)/shard_map/ppermute | solution.py:22
  296.7 5.6 %collective-permute-start.10 = (f32[512,64]{0,1:T(8,128)S(1)}, f32[512,64]{0,1:T(8,128)S(1)}, u32[]{:S(2)}, u32[]{:S(2)}) collective-permute-start(f32[512,64]{0,1:T(8,128)S(1)} %broadcast_select_fusion), channel_id=1, source_target_pairs={{0,2},{1,3},{2,4},{3,5},{4,6},{5,7},{6,8},{7,9},{8,10},{9,11},{10,... | collective-permute-start | bytes 393224 | tf_op jit(solution)/shard_map/ppermute | solution.py:22
  301.0 6.5 %collective-permute-start.8 = (f32[512,64]{0,1:T(8,128)S(1)}, f32[512,64]{0,1:T(8,128)S(1)}, u32[]{:S(2)}, u32[]{:S(2)}) collective-permute-start(f32[512,64]{0,1:T(8,128)S(1)} %broadcast_select_fusion.1), channel_id=1, source_target_pairs={{2,0},{3,1},{4,2},{5,3},{6,4},{7,5},{8,6},{9,7},{10,8},{11,9},{12,... | collective-permute-start | bytes 393224 | tf_op jit(solution)/shard_map/ppermute | solution.py:22
where the time goes:
time: 342 us
  waiting for transfers between devices  151 us (44%)
  blocking collectives  90.7 us (27%)
  starting transfers between devices  78.2 us (23%)
  other arithmetic  9.87 us (3%)
  matrix products  9.11 us (3%)
    ppermute x11, waiting for transfers between devices, from_behind(): return lax.ppermute(block, axis, route)  117 us
    all_to_all x6, blocking collectives, sent_to_all(): return lax.all_to_all(copies, axis, split_axis=0, concat_axis=0, tiled=True)  90.7 us
    ppermute x11, starting transfers between devices, from_behind(): return lax.ppermute(block, axis, route)  68.3 us
    all_to_all x1, waiting for transfers between devices, summed_on_arrival(): lax.all_to_all(parts, axis, split_axis=0, concat_axis=0, tiled=True)  24.7 us
    all_to_all x1, waiting for transfers between devices, sent_to_all(): return lax.all_to_all(copies, axis, split_axis=0, concat_axis=0, tiled=True)  9.32 us
  transfers between devices with their start and end apart: 13, of which 10 were waited for; matrix products, arithmetic and copies ran while one was open for 2% of the time, Pallas kernels for 0%

commit v1 on v0

v1 whole, which is shorter than its diff:
```python
import functools

import jax
import jax.numpy as jnp
from jax import lax
from jax.experimental import pallas as pl
from jax.experimental.pallas import tpu as pltpu
from jax.sharding import PartitionSpec as P

MESH = pl.DeviceIdType.MESH
CHUNKS = 4
LINE = 16


def two_parts(x):
    high = x.astype(jnp.bfloat16)
    low = (x - high.astype(jnp.float32)).astype(jnp.bfloat16)
    return jnp.concatenate([high, low], 0)


def lanes_to_row(x):
    width = x.shape[1]
    total = x[:, 0:128]
    for start in range(128, width, 128):
        total = total + x[:, start : start + 128]
    return jnp.sum(total.T, axis=0, keepdims=True)


def kernel(
    n_samp, n_snp, line, samples,
    dosage, width, marginal, penalty,
    effects, residual,
    grid, marg, stats, widths, vec_t, own, own_f32, near, part, fold, fold_in,
    tile_a, tile_b, factors,
    load_sem, marg_sem, stat_send, stat_recv, width_send, width_recv,
    u_send, u_recv, fold_send, fold_recv, a_send, a_recv, b_send, b_recv,
):
    chunk = grid.shape[1]
    block = grid.shape[2]
    traits = vec_t.shape[0]
    half = traits // 2
    y = lax.axis_index("samp")
    i = lax.axis_index("snp")
    core = lax.rem(i, 2)
    side = 2 * core - 1

    def snp_at(step):
        return lax.rem(i + step + n_snp, n_snp)

    def samp_at(step):
        return lax.rem(y + step, n_samp)

    loads = []
    for k in range(CHUNKS):
        copy = pltpu.make_async_copy(
            dosage.at[pl.ds(k * chunk, chunk), :], grid.at[k], load_sem.at[k]
        )
        copy.start()
        loads.append(copy)
    marg_copy = pltpu.make_async_copy(marginal, marg, marg_sem)
    marg_copy.start()

    spot = lax.rem(i, line)
    base = i - spot
    line_peers = [(y, base + lax.rem(spot + d, line)) for d in range(1, line)]
    n_lines = n_snp // line
    plane_peers = []
    for dx in range(n_lines):
        for dy in range(n_samp):
            if dx or dy:
                plane_peers.append((samp_at(dy), lax.rem(i + line * dx, n_snp)))
    near_peers = [(y, snp_at(d)) for d in (-3, -2, -1, 1, 2, 3)]
    barrier = pltpu.get_barrier_semaphore()
    everyone = near_peers + line_peers + plane_peers
    for peer in everyone:
        pl.semaphore_signal(barrier, inc=1, device_id=peer, device_id_type=MESH)

    def send(src, dst, send_sem, recv_sem, peer):
        return pltpu.make_async_remote_copy(
            src_ref=src, dst_ref=dst, send_sem=send_sem, recv_sem=recv_sem,
            device_id=peer, device_id_type=MESH,
        )

    own_width = width[0].astype(jnp.float32)
    widths[0] = jnp.full(widths.shape[1:], own_width, jnp.float32)
    rows = 64
    sums = (jnp.zeros((8, block), jnp.float32), jnp.zeros((8, block), jnp.float32))
    for k in range(CHUNKS):
        loads[k].wait()

        def add_rows(r, carry, k=k):
            first, second = carry
            g = grid[k, pl.ds(pl.multiple_of(r * rows, rows), rows), :].astype(jnp.float32)
            g = g.reshape(rows // 8, 8, block)
            return first + jnp.sum(g, 0), second + jnp.sum(g * g, 0)

        sums = lax.fori_loop(0, chunk // rows, add_rows, sums)
    stats[0, 0:1, :] = jnp.sum(sums[0], 0, keepdims=True)
    stats[0, 1:2, :] = jnp.sum(sums[1], 0, keepdims=True)

    pl.semaphore_wait(barrier, len(everyone))

    started = []
    stat_copies = []
    for d in range(1, n_samp):
        copy = send(
            stats.at[0], stats.at[d], stat_send.at[d - 1], stat_recv.at[d - 1],
            (samp_at(d), i),
        )
        copy.start()
        stat_copies.append(copy)
    width_copies = []
    for d in (1, 2, 3):
        copy = send(
            widths.at[0], widths.at[d], width_send.at[d - 1], width_recv.at[d - 1],
            (y, snp_at(d)),
        )
        copy.start()
        width_copies.append(copy)

    marg_copy.wait()
    vec_t[...] = marg[...]
    m0 = lanes_to_row(marg[...] * marg[...])
    vector = two_parts(marg[...])

    for copy in stat_copies:
        copy.wait_recv()
    first = (stats[0] + stats[2]) + (stats[1] + stats[3])
    center = first[0:1, :] / samples
    spread = first[1:2, :] / samples - center * center
    scale = lax.rsqrt(spread + 1e-05)

    partner = (y, snp_at(-side))
    forth = (y, snp_at(2 * side))
    back = (y, snp_at(-2 * side))
    outer = (y, snp_at(side))

    masks = {}

    def make_masks():
        for copy in width_copies:
            copy.wait_recv()
        right = {}
        left = {}
        for d in (1, 2, 3):
            allowed = jnp.where(widths[0][0:1, 0:1] >= d, 1.0, 0.0)
            inside = jnp.where(i + d < n_snp, 1.0, 0.0)
            right[d] = allowed * inside
            allowed = jnp.where(widths[d][0:1, 0:1] >= d, 1.0, 0.0)
            inside = jnp.where(i - d >= 0, 1.0, 0.0)
            left[d] = allowed * inside
        turn = jnp.where(core == 1, 1.0, 0.0)
        for d in (1, 2, 3):
            masks["in", d] = turn * left[d] + (1.0 - turn) * right[d]
            masks["out", d] = turn * right[d] + (1.0 - turn) * left[d]

    order = ((0, ("in", 1)), (1, ("in", 2)), (2, ("in", 3)),
             (3, ("out", 1)), (4, ("out", 2)), (5, ("out", 3)))

    def fold_copy(p, leg, piece, peer):
        cut = pl.ds(piece * half, half)
        source = part.at[p] if leg == 0 else fold.at[p]
        return send(
            source.at[cut], fold_in.at[p, leg, cut],
            fold_send.at[p, leg, piece], fold_recv.at[p, leg, piece], peer,
        )

    flipped = y + 1 - 2 * lax.rem(y, 2)
    mirrored = n_samp - 1 - y
    images = []
    trail = None
    cross = []
    for p in range(2):
        moves = []
        for k in range(CHUNKS):
            if p == 0:
                def standardize(r, carry, k=k):
                    cut = pl.ds(pl.multiple_of(r * rows, rows), rows)
                    g = grid[k, cut, :].astype(jnp.float32)
                    grid[k, cut, :] = ((g - center) * scale).astype(jnp.bfloat16)
                    return carry

                lax.fori_loop(0, chunk // rows, standardize, 0)
            u = lax.dot_general(
                vector, grid[k], (((1,), (1,)), ((), ())),
                preferred_element_type=jnp.float32,
            )
            u = u[:traits] + u[traits:]
            own_f32[k] = u
            own[p, k] = u.astype(jnp.bfloat16)
            here = []
            for leg, (slot, peer) in enumerate(((1, forth), (4, back), (0, partner))):
                copy = send(
                    own.at[p, k], near.at[p, slot, k],
                    u_send.at[p, slot, k], u_recv.at[p, slot, k], peer,
                )
                copy.start()
                here.append(copy)
            moves.append(here)
        if p == 0:
            make_masks()
        passed = []
        for k in range(CHUNKS):
            inward, outward, beside = moves[k]
            inward.wait_recv()
            relay = send(
                near.at[p, 1, k], near.at[p, 5, k],
                u_send.at[p, 5, k], u_recv.at[p, 5, k], outer,
            )
            relay.start()
            to_one = send(
                near.at[p, 1, k], near.at[p, 3, k],
                u_send.at[p, 3, k], u_recv.at[p, 3, k], partner,
            )
            to_one.start()
            outward.wait_recv()
            to_three = send(
                near.at[p, 4, k], near.at[p, 2, k],
                u_send.at[p, 2, k], u_recv.at[p, 2, k], partner,
            )
            to_three.start()
            passed.append((to_one, to_three, relay))
        total = jnp.zeros((2 * traits, block), jnp.float32)
        for k in range(CHUNKS):
            moves[k][2].wait_recv()
            for copy in passed[k]:
                copy.wait_recv()
            u = own_f32[k]
            w = u
            for slot, key in order:
                w = w + masks[key] * near[p, slot, k].astype(jnp.float32)
            if p == 1:
                piece = u * w
                folded = piece[:, 0:128]
                for start in range(128, chunk, 128):
                    folded = folded + piece[:, start : start + 128]
                cross.append(folded)
            total = total + lax.dot_general(
                two_parts(w), grid[k], (((1,), (0,)), ((), ())),
                preferred_element_type=jnp.float32,
            )
        part[p] = (total[:traits] + total[traits:]) * (1.0 / samples)
        legs = [fold_copy(p, 0, 0, (flipped, i)), fold_copy(p, 0, 1, (mirrored, i))]
        for copy in legs:
            copy.start()
        if p == 1:
            m3 = lanes_to_row(cross[0] + cross[1] + cross[2] + cross[3]) * (1.0 / samples)
            tile_a[spot] = jnp.zeros(tile_a.shape[1:], jnp.float32)
            share = 1.0 / n_samp
            tile_a[spot, 0:1, 0:traits] = m0 * share
            tile_a[spot, 1:2, 0:traits] = m1 * share
            tile_a[spot, 2:3, 0:traits] = m2 * share
            tile_a[spot, 3:4, 0:traits] = m3
            line_copies = []
            for d, peer in enumerate(line_peers):
                copy = send(
                    tile_a.at[spot], tile_a.at[spot], a_send.at[d], a_recv.at[d], peer
                )
                copy.start()
                line_copies.append(copy)
        for copy in legs:
            copy.wait_recv()
        fold[p] = part[p] + fold_in[p, 0]
        legs_b = [fold_copy(p, 1, 0, (mirrored, i)), fold_copy(p, 1, 1, (flipped, i))]
        for copy in legs_b:
            copy.start()
        if p == 1:
            for copy in line_copies:
                copy.wait_recv()
            summed = tile_a[0]
            for q in range(1, line):
                summed = summed + tile_a[q]
            seat = (i // line) * n_samp + y
            tile_b[seat] = summed
            plane_copies = []
            for d, peer in enumerate(plane_peers):
                copy = send(
                    tile_b.at[seat], tile_b.at[seat], b_send.at[d], b_recv.at[d], peer
                )
                copy.start()
                plane_copies.append(copy)
        for copy in legs_b:
            copy.wait_recv()
        image = fold[p] + fold_in[p, 1] - vec_t[...]
        if p == 0:
            m1 = lanes_to_row(vec_t[...] * image)
            m2 = lanes_to_row(image * image)
            vec_t[...] = image
            vector = two_parts(image)
        images.append(image)
        for group in moves + passed + [legs, legs_b]:
            for copy in group:
                started.append(copy)
    for copy in plane_copies:
        copy.wait_recv()
    summed = tile_b[0]
    for q in range(1, n_lines * n_samp):
        summed = summed + tile_b[q]
    m0 = summed[0:1, 0:traits]
    m1 = summed[1:2, 0:traits]
    m2 = summed[2:3, 0:traits]
    m3 = summed[3:4, 0:traits] - m2
    tau = penalty[...] + 1.0
    mu1 = tau * m0 + m1
    alpha0 = m0 / mu1
    g = m1 / mu1
    rr1 = alpha0 * alpha0 * m2 - g * g * m0
    beta0 = rr1 / m0
    inner = g * g * m1 - 2.0 * g * alpha0 * m2 + alpha0 * alpha0 * m3
    curve = tau * rr1 + inner - beta0 * rr1 / alpha0
    alpha1 = rr1 / curve
    lead = g + beta0
    b = marg[...]
    p1, p2 = images
    factors[...] = jnp.zeros_like(factors)
    factors[0:1, 0:traits] = alpha0 + alpha1 * lead
    factors[1:2, 0:traits] = alpha1 * alpha0
    factors[2:3, 0:traits] = g - alpha1 * lead * tau
    factors[3:4, 0:traits] = alpha1 * (alpha0 * tau - lead) - alpha0
    columns = factors[...].T
    e_b, cross_term, r_b, r_p1 = (columns[:traits, q : q + 1] for q in range(4))
    effects[...] = e_b * b - cross_term * p1
    residual[...] = r_b * b + r_p1 * p1 + cross_term * p2
    for copy in started + stat_copies + width_copies + line_copies + plane_copies:
        copy.wait_send()


def solution(mesh):
    n_samp, n_snp = mesh.shape["samp"], mesh.shape["snp"]
    line = min(LINE, n_snp // 2)

    def step(dosage, band_width, marginal, penalty):
        mine, block = dosage.shape
        traits = marginal.shape[1]
        chunk = mine // CHUNKS
        seats = n_samp * n_snp // line
        dma = pltpu.SemaphoreType.DMA
        f32, bf16 = jnp.float32, jnp.bfloat16
        anywhere = pl.BlockSpec(memory_space=pl.ANY)
        vmem = pl.BlockSpec(memory_space=pltpu.VMEM)
        shape = jax.ShapeDtypeStruct((traits, block), f32)
        effects, residual = pl.pallas_call(
            functools.partial(kernel, n_samp, n_snp, line, mine * n_samp),
            out_shape=(shape, shape),
            in_specs=[anywhere, pl.BlockSpec(memory_space=pltpu.SMEM), anywhere, vmem],
            out_specs=(vmem, vmem),
            scratch_shapes=[
                pltpu.VMEM((CHUNKS, chunk, block), bf16),
                pltpu.VMEM((traits, block), f32),
                pltpu.VMEM((n_samp, 2, block), f32),
                pltpu.VMEM((4, 8, 128), f32),
                pltpu.VMEM((traits, block), f32),
                pltpu.VMEM((2, CHUNKS, traits, chunk), bf16),
                pltpu.VMEM((CHUNKS, traits, chunk), f32),
                pltpu.VMEM((2, 6, CHUNKS, traits, chunk), bf16),
                pltpu.VMEM((2, traits, block), f32),
                pltpu.VMEM((2, traits, block), f32),
                pltpu.VMEM((2, 2, traits, block), f32),
                pltpu.VMEM((line, 8, 128), f32),
                pltpu.VMEM((seats, 8, 128), f32),
                pltpu.VMEM((8, 128), f32),
                dma((CHUNKS,)),
                dma,
                dma((n_samp - 1,)), dma((n_samp - 1,)),
                dma((3,)), dma((3,)),
                dma((2, 6, CHUNKS)), dma((2, 6, CHUNKS)),
                dma((2, 2, 2)), dma((2, 2, 2)),
                dma((line - 1,)), dma((line - 1,)),
                dma((seats - 1,)), dma((seats - 1,)),
            ],
            compiler_params=pltpu.CompilerParams(
                collective_id=0, has_side_effects=True,
                vmem_limit_bytes=60 * 1024 * 1024,
            ),
        )(dosage, band_width, marginal.T, penalty[None, :])
        return effects.T, residual.T

    in_specs = (P("samp", "snp"), P("snp"), P("snp", None), P())
    out_specs = (P("snp", None), P("snp", None))
    return jax.shard_map(step, mesh=mesh, in_specs=in_specs, out_specs=out_specs, check_vma=False)
```

time: 342 us -> 61.5 us (0.18)
  waiting for transfers between devices: 151 us -> 0 us
  blocking collectives: 90.7 us -> 0 us
  starting transfers between devices: 78.2 us -> 0 us
  Pallas kernels: 0 us -> 56.9 us
  other arithmetic: 9.87 us -> 0 us
  matrix products: 9.11 us -> 0 us
    ppermute x11 -> x0, waiting for transfers between devices: 117 us -> none  [from_behind(): return lax.ppermute(block, axis, route)]
    all_to_all x6 -> x0, blocking collectives: 90.7 us -> none  [sent_to_all(): return lax.all_to_all(copies, axis, split_axis=0, concat_axis=0, tiled=True)]
    ppermute x11 -> x0, starting transfers between devices: 68.3 us -> none  [from_behind(): return lax.ppermute(block, axis, route)]
    pallas_call x0 -> x1, Pallas kernels: none -> 56.9 us  [step(): pl.pallas_call(functools.partial(kernel, n_samp, n_snp, line, mine * n_sa...]
    all_to_all x2 -> x0, waiting for transfers between devices: 34 us -> none  [the longest x1 24.7 us: summed_on_arrival(): lax.all_to_all(parts, axis, split_axis=0, concat_axis=0, tiled=True)]
    all_to_all x2 -> x0, starting transfers between devices: 9.86 us -> none  [the longest x1 4.99 us: summed_on_arrival(): lax.all_to_all(parts, axis, split_axis=0, concat_axis=0, tiled=True)]
    dot_general x8 -> x0, matrix products: 9.11 us -> none  [the longest x4 5.17 us: gram_pair(): lax.dot_general(scaled, other, (((0,), (0,)), ((), ())), preferred_elemen...]
    reduce_sum x12 -> x0, other arithmetic: 5.88 us -> none  [the longest x1 2.78 us: summed_on_arrival(): return arrived.sum(axis=0)]
  transfers between devices with their start and end apart: 13 -> 0, of which waited for: 10 -> 0; matrix products, arithmetic and copies ran while one was open for 2% -> 0% of each run, Pallas kernels for 0% -> 0%
where the time goes in v1:
time: 61.5 us; the launch traced here: 61.3 us
  Pallas kernels  56.9 us (93%)
  local copies, waits for them, and re-layouts  3.14 us (5%)
  between operations  1.28 us (2%)
    pallas_call x1, Pallas kernels, step(): pl.pallas_call(functools.partial(kernel, n_samp, n_snp, line, mine * n_sa...  56.9 us
    unnamed x2, local copies, waits for them, and re-layouts  3.14 us

profile of v1, /device:TPU:1, one launch (start us, length us, event | category | flops | bytes accessed | tf_op | source)
XLA Modules:
  0.0 61.3 jit_solution(9313556199834293780)
XLA Ops:
  1.3 56.9 %shard_map.59 = (f32[64,512]{1,0:T(8,128)}, f32[64,512]{1,0:T(8,128)}) custom-call(bf16[2048,512]{1,0:T(8,128)(2,1)} %dosage.1, s32[1]{0:T(128)S(6)} %copy.8.width, f32[64,512]{1,0:T(8,128)} %bitcast.4, f32[1,64]{1,0:T(1,128)} %bitcast.7), custom_call_target="tpu_custom_call" | custom-call | tf_op jit(solution)/shard_map/pallas_call | solution.py:342
  58.2 1.6 %copy.9 = f32[512,64]{0,1:T(8,128)} copy(f32[512,64]{0,1:T(8,128)} %bitcast.6) | data formatting | bytes 262144
  59.7 1.6 %copy.10 = f32[512,64]{0,1:T(8,128)} copy(f32[512,64]{0,1:T(8,128)} %bitcast.5) | data formatting | bytes 262144

commit v2 on v1

--- a/solution.py
+++ b/solution.py
@@ -10,6 +10,8 @@
 MESH = pl.DeviceIdType.MESH
 CHUNKS = 4
 LINE = 16
+GRANT = 56203674
+REACH = (2, 3, 6)
 
 
 def two_parts(x):
@@ -28,10 +30,10 @@
 
 def kernel(
     n_samp, n_snp, line, samples,
-    dosage, width, marginal, penalty,
-    effects, residual,
+    dosage, width_hbm, marginal,
+    first_image, second_image, coefs,
     grid, marg, stats, widths, vec_t, own, own_f32, near, part, fold, fold_in,
-    tile_a, tile_b, factors,
+    tile_a, tile_b, width, width_sem,
     load_sem, marg_sem, stat_send, stat_recv, width_send, width_recv,
     u_send, u_recv, fold_send, fold_recv, a_send, a_recv, b_send, b_recv,
 ):
@@ -59,6 +61,8 @@
         loads.append(copy)
     marg_copy = pltpu.make_async_copy(marginal, marg, marg_sem)
     marg_copy.start()
+    width_copy = pltpu.make_async_copy(width_hbm, width, width_sem)
+    width_copy.start()
 
     spot = lax.rem(i, line)
     base = i - spot
@@ -71,7 +75,13 @@
                 plane_peers.append((samp_at(dy), lax.rem(i + line * dx, n_snp)))
     near_peers = [(y, snp_at(d)) for d in (-3, -2, -1, 1, 2, 3)]
     barrier = pltpu.get_barrier_semaphore()
-    everyone = near_peers + line_peers + plane_peers
+    y_peers = [(samp_at(d), i) for d in range(1, n_samp)]
+    x_peers = [(y, lax.rem(i + line * d, n_snp)) for d in range(1, n_lines)]
+    far_steps = [d for d in REACH if 2 * d <= line]
+    far_peers = [
+        (y, base + lax.rem(spot + e, line)) for d in far_steps for e in (d, line - d)
+    ]
+    everyone = near_peers + y_peers + x_peers + far_peers
     for peer in everyone:
         pl.semaphore_signal(barrier, inc=1, device_id=peer, device_id_type=MESH)
 
@@ -81,6 +91,7 @@
             device_id=peer, device_id_type=MESH,
         )
 
+    width_copy.wait()
     own_width = width[0].astype(jnp.float32)
     widths[0] = jnp.full(widths.shape[1:], own_width, jnp.float32)
     rows = 64
@@ -199,6 +210,9 @@
             moves.append(here)
         if p == 0:
             make_masks()
+        else:
+            m1 = lanes_to_row(marg[...] * images[0])
+            m2 = lanes_to_row(images[0] * images[0])
         passed = []
         for k in range(CHUNKS):
             inward, outward, beside = moves[k]
@@ -235,6 +249,21 @@
                 for start in range(128, chunk, 128):
                     folded = folded + piece[:, start : start + 128]
                 cross.append(folded)
+            if p == 1 and k == CHUNKS - 1:
+                m3 = lanes_to_row(sum(cross[1:], cross[0])) * (1.0 / samples)
+                tile_a[spot] = jnp.zeros(tile_a.shape[1:], jnp.float32)
+                share = 1.0 / n_samp
+                tile_a[spot, 0:1, 0:traits] = m0 * share
+                tile_a[spot, 1:2, 0:traits] = m1 * share
+                tile_a[spot, 2:3, 0:traits] = m2 * share
+                tile_a[spot, 3:4, 0:traits] = m3
+                line_copies = []
+                for d, peer in enumerate(line_peers):
+                    copy = send(
+                        tile_a.at[spot], tile_a.at[spot], a_send.at[d], a_recv.at[d], peer
+                    )
+                    copy.start()
+                    line_copies.append(copy)
             total = total + lax.dot_general(
                 two_parts(w), grid[k], (((1,), (0,)), ((), ())),
                 preferred_element_type=jnp.float32,
@@ -243,21 +272,6 @@
         legs = [fold_copy(p, 0, 0, (flipped, i)), fold_copy(p, 0, 1, (mirrored, i))]
         for copy in legs:
             copy.start()
-        if p == 1:
-            m3 = lanes_to_row(cross[0] + cross[1] + cross[2] + cross[3]) * (1.0 / samples)
-            tile_a[spot] = jnp.zeros(tile_a.shape[1:], jnp.float32)
-            share = 1.0 / n_samp
-            tile_a[spot, 0:1, 0:traits] = m0 * share
-            tile_a[spot, 1:2, 0:traits] = m1 * share
-            tile_a[spot, 2:3, 0:traits] = m2 * share
-            tile_a[spot, 3:4, 0:traits] = m3
-            line_copies = []
-            for d, peer in enumerate(line_peers):
-                copy = send(
-                    tile_a.at[spot], tile_a.at[spot], a_send.at[d], a_recv.at[d], peer
-                )
-                copy.start()
-                line_copies.append(copy)
         for copy in legs:
             copy.wait_recv()
         fold[p] = part[p] + fold_in[p, 0]
@@ -283,10 +297,8 @@
             copy.wait_recv()
         image = fold[p] + fold_in[p, 1] - vec_t[...]
         if p == 0:
-            m1 = lanes_to_row(vec_t[...] * image)
-            m2 = lanes_to_row(image * image)
+            vector = two_parts(image)
             vec_t[...] = image
-            vector = two_parts(image)
         images.append(image)
         for group in moves + passed + [legs, legs_b]:
             for copy in group:
@@ -296,31 +308,10 @@
     summed = tile_b[0]
     for q in range(1, n_lines * n_samp):
         summed = summed + tile_b[q]
-    m0 = summed[0:1, 0:traits]
-    m1 = summed[1:2, 0:traits]
-    m2 = summed[2:3, 0:traits]
-    m3 = summed[3:4, 0:traits] - m2
-    tau = penalty[...] + 1.0
-    mu1 = tau * m0 + m1
-    alpha0 = m0 / mu1
-    g = m1 / mu1
-    rr1 = alpha0 * alpha0 * m2 - g * g * m0
-    beta0 = rr1 / m0
-    inner = g * g * m1 - 2.0 * g * alpha0 * m2 + alpha0 * alpha0 * m3
-    curve = tau * rr1 + inner - beta0 * rr1 / alpha0
-    alpha1 = rr1 / curve
-    lead = g + beta0
-    b = marg[...]
+    coefs[...] = summed
     p1, p2 = images
-    factors[...] = jnp.zeros_like(factors)
-    factors[0:1, 0:traits] = alpha0 + alpha1 * lead
-    factors[1:2, 0:traits] = alpha1 * alpha0
-    factors[2:3, 0:traits] = g - alpha1 * lead * tau
-    factors[3:4, 0:traits] = alpha1 * (alpha0 * tau - lead) - alpha0
-    columns = factors[...].T
-    e_b, cross_term, r_b, r_p1 = (columns[:traits, q : q + 1] for q in range(4))
-    effects[...] = e_b * b - cross_term * p1
-    residual[...] = r_b * b + r_p1 * p1 + cross_term * p2
+    first_image[...] = p1
+    second_image[...] = p2
     for copy in started + stat_copies + width_copies + line_copies + plane_copies:
         copy.wait_send()
 
@@ -339,11 +330,11 @@
         anywhere = pl.BlockSpec(memory_space=pl.ANY)
         vmem = pl.BlockSpec(memory_space=pltpu.VMEM)
         shape = jax.ShapeDtypeStruct((traits, block), f32)
-        effects, residual = pl.pallas_call(
+        p1, p2, coefs = pl.pallas_call(
             functools.partial(kernel, n_samp, n_snp, line, mine * n_samp),
-            out_shape=(shape, shape),
-            in_specs=[anywhere, pl.BlockSpec(memory_space=pltpu.SMEM), anywhere, vmem],
-            out_specs=(vmem, vmem),
+            out_shape=(shape, shape, jax.ShapeDtypeStruct((8, 128), f32)),
+            in_specs=[anywhere, anywhere, anywhere],
+            out_specs=(vmem, vmem, vmem),
             scratch_shapes=[
                 pltpu.VMEM((CHUNKS, chunk, block), bf16),
                 pltpu.VMEM((traits, block), f32),
@@ -358,7 +349,8 @@
                 pltpu.VMEM((2, 2, traits, block), f32),
                 pltpu.VMEM((line, 8, 128), f32),
                 pltpu.VMEM((seats, 8, 128), f32),
-                pltpu.VMEM((8, 128), f32),
+                pltpu.SMEM((1,), jnp.int32),
+                dma,
                 dma((CHUNKS,)),
                 dma,
                 dma((n_samp - 1,)), dma((n_samp - 1,)),
@@ -370,9 +362,29 @@
             ],
             compiler_params=pltpu.CompilerParams(
                 collective_id=0, has_side_effects=True,
-                vmem_limit_bytes=60 * 1024 * 1024,
+                vmem_limit_bytes=GRANT,
             ),
-        )(dosage, band_width, marginal.T, penalty[None, :])
+        )(dosage, band_width, marginal.T)
+        m0, m1, m2, mixed = (coefs[q, :traits] for q in range(4))
+        m3 = mixed - m2
+        tau = penalty + 1.0
+        mu1 = tau * m0 + m1
+        alpha0 = m0 / mu1
+        g = m1 / mu1
+        rr1 = alpha0 * alpha0 * m2 - g * g * m0
+        beta0 = rr1 / m0
+        inner = g * g * m1 - 2.0 * g * alpha0 * m2 + alpha0 * alpha0 * m3
+        curve = tau * rr1 + inner - beta0 * rr1 / alpha0
+        alpha1 = rr1 / curve
+        lead = g + beta0
+        cross = alpha1 * alpha0
+        b = marginal.T
+        effects = (alpha0 + alpha1 * lead)[:, None] * b - cross[:, None] * p1
+        residual = (
+            (g - alpha1 * lead * tau)[:, None] * b
+            + (cross * tau - alpha1 * lead - alpha0)[:, None] * p1
+            + cross[:, None] * p2
+        )
         return effects.T, residual.T
 
     in_specs = (P("samp", "snp"), P("snp"), P("snp", None), P())

time: 61.5 us -> 56.8 us (0.924)
  local copies, waits for them, and re-layouts: 3.14 us -> 0.01 us
  Pallas kernels: 56.9 us -> 54.5 us
  other arithmetic: 0 us -> 0.86 us
    unnamed x2 -> x4, local copies, waits for them, and re-layouts: 3.14 us -> 0.01 us
    pallas_call x1, Pallas kernels: 56.9 us -> 54.5 us  [step(): pl.pallas_call(functools.partial(kernel, n_samp, n_snp, line, mine * n_sa...]
    transpose x0 -> x1, other arithmetic: none -> 0.82 us  [step(): return (effects.T, residual.T)]
where the time goes in v2:
time: 56.8 us; the launch traced here: 56.7 us
  Pallas kernels  54.5 us (96%)
  between operations  1.37 us (2%)
  other arithmetic  0.86 us (2%)
    pallas_call x1, Pallas kernels, step(): pl.pallas_call(functools.partial(kernel, n_samp, n_snp, line, mine * n_sa...  54.5 us

profile of v2, /device:TPU:1, one launch (start us, length us, event | category | flops | bytes accessed | tf_op | source)
XLA Modules:
  0.0 56.7 jit_solution(9392803727931169338)
XLA Ops:
  0.6 0.0 copy-start.1
  0.6 0.0 copy-start
  1.3 54.5 %shard_map.59 = (f32[64,512]{1,0:T(8,128)S(1)}, f32[64,512]{1,0:T(8,128)S(1)}, f32[8,128]{1,0:T(8,128)S(1)}) custom-call(bf16[2048,512]{1,0:T(8,128)(2,1)} %dosage.1, s32[1]{0:T(128)S(6)} %copy.6.width_hbm, f32[64,512]{1,0:T(8,128)} %bitcast.67), custom_call_target="tpu_custom_call" | custom-call | tf_op jit(solution)/shard_map/pallas_call | solution.py:333
  55.8 0.0 copy-done.1
  55.9 0.0 copy-done
  55.9 0.8 %add_bitcast_fusion = (f32[512,64]{0,1:T(8,128)}, f32[512,64]{0,1:T(8,128)}) fusion(f32[64,512]{1,0:T(8,128)S(1)} %get-tuple-element.7, f32[64,512]{1,0:T(8,128)S(1)} %get-tuple-element.6, f32[64]{0:T(128)S(1)} %get-tuple-element.11, f32[64]{0:T(128)S(1)} %get-tuple-element.8, f32[64]{0:T(128)S(1)} %get-tuple-element.12, f32[512,64]{0,1:T(8,128)S(1)} %copy-done, ...), kind=kLoop, calls=%fused_computation | loop fusion | flops 262144 | bytes 656384 | tf_op jit(solution)/shard_map/transpose | solution.py:388
  (3 shorter events, 0.0 us)
Async XLA Ops:
  0.6 55.2 %copy-start.1 = (f32[64]{0:T(128)S(1)}, f32[64]{0:T(128)}, u32[]{:S(2)}) copy-start(f32[64]{0:T(128)} %param.7) | copy-start | bytes 772
  0.6 55.2 %copy-start = (f32[512,64]{0,1:T(8,128)S(1)}, f32[512,64]{0,1:T(8,128)}, u32[]{:S(2)}) copy-start(f32[512,64]{0,1:T(8,128)} %param.6) | copy-start | bytes 393220

commit v3 on v2

v3 whole, which is shorter than its diff:
```python
import functools

import jax
import jax.numpy as jnp
from jax import lax
from jax.experimental import pallas as pl
from jax.experimental.pallas import tpu as pltpu
from jax.sharding import PartitionSpec as P

MESH = pl.DeviceIdType.MESH
CHUNKS = 1
LINE = 16
PARTS = 2
TAIL = 128
GRANT = 56203674
REACH = (2, 3, 6)


def two_parts(x):
    high = x.astype(jnp.bfloat16)
    low = (x - high.astype(jnp.float32)).astype(jnp.bfloat16)
    return jnp.concatenate([high, low], 0)


def lanes_to_row(x):
    width = x.shape[1]
    total = x[:, 0:128]
    for start in range(128, width, 128):
        total = total + x[:, start : start + 128]
    return jnp.sum(total.T, axis=0, keepdims=True)


def kernel(
    n_samp, n_snp, line, samples,
    dosage, width_hbm, marginal,
    first_image, second_image, coefs,
    grid, marg, stats, widths, own, own_f32, near, part, fold, fold_in,
    tile_a, tile_b, width, width_sem,
    load_sem, marg_sem, stat_send, stat_recv, width_send, width_recv,
    u_send, u_recv, fold_send, fold_recv, a_send, a_recv, b_send, b_recv,
):
    chunk = grid.shape[1]
    block = grid.shape[2]
    traits = marg.shape[0]
    half = own.shape[3]
    y = lax.axis_index("samp")
    i = lax.axis_index("snp")
    core = lax.rem(i, 2)
    side = 2 * core - 1

    def snp_at(step):
        return lax.rem(i + step + n_snp, n_snp)

    def samp_at(step):
        return lax.rem(y + step, n_samp)

    loads = []
    for k in range(CHUNKS):
        copy = pltpu.make_async_copy(
            dosage.at[pl.ds(k * chunk, chunk), :], grid.at[k], load_sem.at[k]
        )
        copy.start()
        loads.append(copy)
    marg_copy = pltpu.make_async_copy(marginal, marg, marg_sem)
    marg_copy.start()
    width_copy = pltpu.make_async_copy(width_hbm, width, width_sem)
    width_copy.start()

    spot = lax.rem(i, line)
    base = i - spot
    line_peers = [(y, base + lax.rem(spot + d, line)) for d in range(1, line)]
    n_lines = n_snp // line
    plane_peers = []
    for dx in range(n_lines):
        for dy in range(n_samp):
            if dx or dy:
                plane_peers.append((samp_at(dy), lax.rem(i + line * dx, n_snp)))
    near_peers = [(y, snp_at(d)) for d in (-3, -2, -1, 1, 2, 3)]
    barrier = pltpu.get_barrier_semaphore()
    y_peers = [(samp_at(d), i) for d in range(1, n_samp)]
    x_peers = [(y, lax.rem(i + line * d, n_snp)) for d in range(1, n_lines)]
    far_steps = [d for d in REACH if 2 * d <= line]
    far_peers = [
        (y, base + lax.rem(spot + e, line)) for d in far_steps for e in (d, line - d)
    ]
    everyone = near_peers + y_peers + x_peers + far_peers
    for peer in everyone:
        pl.semaphore_signal(barrier, inc=1, device_id=peer, device_id_type=MESH)

    def send(src, dst, send_sem, recv_sem, peer):
        return pltpu.make_async_remote_copy(
            src_ref=src, dst_ref=dst, send_sem=send_sem, recv_sem=recv_sem,
            device_id=peer, device_id_type=MESH,
        )

    width_copy.wait()
    own_width = width[0].astype(jnp.float32)
    widths[0] = jnp.full(widths.shape[1:], own_width, jnp.float32)
    rows = 64
    sums = (jnp.zeros((8, block), jnp.float32), jnp.zeros((8, block), jnp.float32))
    for k in range(CHUNKS):
        loads[k].wait()

        def add_rows(r, carry, k=k):
            first, second = carry
            g = grid[k, pl.ds(pl.multiple_of(r * rows, rows), rows), :].astype(jnp.float32)
            g = g.reshape(rows // 8, 8, block)
            return first + jnp.sum(g, 0), second + jnp.sum(g * g, 0)

        sums = lax.fori_loop(0, chunk // rows, add_rows, sums)
    stats[0, 0:1, :] = jnp.sum(sums[0], 0, keepdims=True)
    stats[0, 1:2, :] = jnp.sum(sums[1], 0, keepdims=True)

    pl.semaphore_wait(barrier, len(everyone))

    started = []
    stat_copies = []
    for d in range(1, n_samp):
        copy = send(
            stats.at[0], stats.at[d], stat_send.at[d - 1], stat_recv.at[d - 1],
            (samp_at(d), i),
        )
        copy.start()
        stat_copies.append(copy)
    width_copies = []
    for d in (1, 2, 3):
        copy = send(
            widths.at[0], widths.at[d], width_send.at[d - 1], width_recv.at[d - 1],
            (y, snp_at(d)),
        )
        copy.start()
        width_copies.append(copy)

    marg_copy.wait()
    m0 = lanes_to_row(marg[...] * marg[...])
    vector = two_parts(marg[...])

    for copy in stat_copies:
        copy.wait_recv()
    first = (stats[0] + stats[2]) + (stats[1] + stats[3])
    center = first[0:1, :] / samples
    spread = first[1:2, :] / samples - center * center
    scale = lax.rsqrt(spread + 1e-05)

    partner = (y, snp_at(-side))
    forth = (y, snp_at(2 * side))
    back = (y, snp_at(-2 * side))
    outer = (y, snp_at(side))

    masks = {}

    def make_masks():
        for copy in width_copies:
            copy.wait_recv()
        right = {}
        left = {}
        for d in (1, 2, 3):
            allowed = jnp.where(widths[0][0:1, 0:1] >= d, 1.0, 0.0)
            inside = jnp.where(i + d < n_snp, 1.0, 0.0)
            right[d] = allowed * inside
            allowed = jnp.where(widths[d][0:1, 0:1] >= d, 1.0, 0.0)
            inside = jnp.where(i - d >= 0, 1.0, 0.0)
            left[d] = allowed * inside
        turn = jnp.where(core == 1, 1.0, 0.0)
        for d in (1, 2, 3):
            masks["in", d] = turn * left[d] + (1.0 - turn) * right[d]
            masks["out", d] = turn * right[d] + (1.0 - turn) * left[d]

    order = ((0, ("in", 1)), (1, ("in", 2)), (2, ("in", 3)),
             (3, ("out", 1)), (4, ("out", 2)), (5, ("out", 3)))

    def fold_copy(p, h, leg, piece, peer):
        cut = pl.ds(piece * (half // 2), half // 2)
        source = part.at[p, h] if leg == 0 else fold.at[p, h]
        return send(
            source.at[cut], fold_in.at[p, leg, h, cut],
            fold_send.at[p, leg, h, piece], fold_recv.at[p, leg, h, piece], peer,
        )

    flipped = (y + 1 - 2 * lax.rem(y, 2), i)
    mirrored = (n_samp - 1 - y, i)
    halves = range(traits // half)
    moves, passed, legs = {}, {}, {}
    cross = {}

    def hop(p, h, k, source, slot, peer):
        copy = send(
            source, near.at[p, h, slot, k],
            u_send.at[p, h, slot, k], u_recv.at[p, h, slot, k], peer,
        )
        copy.start()
        return copy

    def send_own(p, h, k):
        moves[p, h, k] = [
            hop(p, h, k, own.at[p, h, k], slot, peer)
            for slot, peer in ((1, forth), (4, back), (0, partner))
        ]

    def project(vector, k):
        u = lax.dot_general(
            vector, grid[k], (((1,), (1,)), ((), ())),
            preferred_element_type=jnp.float32,
        )
        rows_out = vector.shape[0] // 2
        return u[:rows_out] + u[rows_out:]

    def keep(p, h, k, u):
        own_f32[h, k] = u
        peak = jnp.maximum(jnp.max(jnp.abs(u), 1, keepdims=True), 1e-30)
        power = jnp.ceil(jnp.log2(peak * (1.0 / 32000.0)))
        coded = jnp.round(u * jnp.exp2(-power))
        own[p, h, k, :, 0:chunk] = coded.astype(jnp.int32).astype(jnp.int16)
        tail = jnp.broadcast_to(power, (u.shape[0], TAIL))
        own[p, h, k, :, chunk:] = tail.astype(jnp.int32).astype(jnp.int16)

    def forward(p, h):
        for k in range(CHUNKS):
            inward, outward, _ = moves[p, h, k]
            inward.wait_recv()
            relay = hop(p, h, k, near.at[p, h, 1, k], 5, outer)
            to_one = hop(p, h, k, near.at[p, h, 1, k], 3, partner)
            outward.wait_recv()
            to_three = hop(p, h, k, near.at[p, h, 4, k], 2, partner)
            passed[p, h, k] = [to_one, to_three, relay]

    def banded(p, h, k):
        moves[p, h, k][2].wait_recv()
        for copy in passed[p, h, k]:
            copy.wait_recv()
        u = own_f32[h, k]
        w = u
        for slot, key in order:
            coded = near[p, h, slot, k, :, 0:chunk].astype(jnp.int32).astype(jnp.float32)
            power = near[p, h, slot, k, :, chunk:].astype(jnp.int32).astype(jnp.float32)
            w = w + (masks[key] * jnp.exp2(power[:, 0:1])) * coded
        if p == 1:
            piece = u * w
            folded = piece[:, 0:128]
            for start in range(128, chunk, 128):
                folded = folded + piece[:, start : start + 128]
            cross[h] = cross[h] + folded if k else folded
        return two_parts(w)

    def gather_back(w, k):
        return lax.dot_general(
            w, grid[k], (((1,), (0,)), ((), ())), preferred_element_type=jnp.float32
        )

    def apply_band(p, h, before_last):
        total = None
        for k in range(CHUNKS):
            w = banded(p, h, k)
            if k == CHUNKS - 1:
                before_last()
            term = gather_back(w, k)
            total = term if total is None else total + term
        part[p, h] = (total[:half] + total[half:]) * (1.0 / samples)
        legs[p, h, 0] = [fold_copy(p, h, 0, 0, flipped), fold_copy(p, h, 0, 1, mirrored)]
        for copy in legs[p, h, 0]:
            copy.start()

    def fold_once(p, h):
        for copy in legs[p, h, 0]:
            copy.wait_recv()
        fold[p, h] = part[p, h] + fold_in[p, 0, h]
        legs[p, h, 1] = [fold_copy(p, h, 1, 0, mirrored), fold_copy(p, h, 1, 1, flipped)]
        for copy in legs[p, h, 1]:
            copy.start()

    def fold_twice(p, h):
        for copy in legs[p, h, 1]:
            copy.wait_recv()
        return fold[p, h] + fold_in[p, 1, h]

    def trait_cut(h):
        return pl.ds(h * half, half)

    for k in range(CHUNKS):
        def standardize(r, carry, k=k):
            cut = pl.ds(pl.multiple_of(r * rows, rows), rows)
            g = grid[k, cut, :].astype(jnp.float32)
            grid[k, cut, :] = ((g - center) * scale).astype(jnp.bfloat16)
            return carry

        lax.fori_loop(0, chunk // rows, standardize, 0)
        u = project(vector, k)
        for h in halves:
            keep(0, h, k, u[h * half : (h + 1) * half])
        send_own(0, 0, k)
    for h in halves[1:]:
        for k in range(CHUNKS):
            send_own(0, h, k)
    make_masks()
    for h in halves:
        forward(0, h)
    for h in halves:
        apply_band(0, h, lambda: None)
    for h in halves:
        fold_once(0, h)

    for h in halves:
        image = fold_twice(0, h) - marg[trait_cut(h), :]
        first_image[trait_cut(h), :] = image
        vector = two_parts(image)
        for k in range(CHUNKS):
            keep(1, h, k, project(vector, k))
            send_own(1, h, k)
    m1 = lanes_to_row(marg[...] * first_image[...])
    m2 = lanes_to_row(first_image[...] * first_image[...])
    line_copies = []

    def send_sums():
        share = 1.0 / n_samp
        m3 = lanes_to_row(jnp.concatenate([cross[h] for h in halves], 0))
        tile_a[spot, 0:1, :] = jnp.concatenate([m0 * share, m1 * share], 1)
        tile_a[spot, 1:2, :] = jnp.concatenate([m2 * share, m3 * (1.0 / samples)], 1)
        for d, peer in enumerate(line_peers):
            copy = send(
                tile_a.at[spot], tile_a.at[spot], a_send.at[d], a_recv.at[d], peer
            )
            copy.start()
            line_copies.append(copy)

    for h in halves:
        forward(1, h)
    for h in halves:
        apply_band(1, h, send_sums if h == halves[-1] else lambda: None)
    for h in halves:
        fold_once(1, h)
    for copy in line_copies:
        copy.wait_recv()
    summed = tile_a[0]
    for q in range(1, line):
        summed = summed + tile_a[q]
    seat = (i // line) * n_samp + y
    tile_b[seat] = summed
    plane_copies = []
    for d, peer in enumerate(plane_peers):
        copy = send(
            tile_b.at[seat], tile_b.at[seat], b_send.at[d], b_recv.at[d], peer
        )
        copy.start()
        plane_copies.append(copy)
    for h in halves:
        second_image[trait_cut(h), :] = fold_twice(1, h) - first_image[trait_cut(h), :]
    for table in (moves, passed, legs):
        for group in table.values():
            started.extend(group)
    for copy in plane_copies:
        copy.wait_recv()
    summed = tile_b[0]
    for q in range(1, n_lines * n_samp):
        summed = summed + tile_b[q]
    coefs[...] = summed
    for copy in started + stat_copies + width_copies + line_copies + plane_copies:
        copy.wait_send()


def solution(mesh):
    n_samp, n_snp = mesh.shape["samp"], mesh.shape["snp"]
    line = min(LINE, n_snp // 2)

    def step(dosage, band_width, marginal, penalty):
        mine, block = dosage.shape
        traits = marginal.shape[1]
        chunk = mine // CHUNKS
        parts, half = PARTS, traits // PARTS
        seats = n_samp * n_snp // line
        dma = pltpu.SemaphoreType.DMA
        f32, bf16 = jnp.float32, jnp.bfloat16
        anywhere = pl.BlockSpec(memory_space=pl.ANY)
        vmem = pl.BlockSpec(memory_space=pltpu.VMEM)
        shape = jax.ShapeDtypeStruct((traits, block), f32)
        p1, p2, coefs = pl.pallas_call(
            functools.partial(kernel, n_samp, n_snp, line, mine * n_samp),
            out_shape=(shape, shape, jax.ShapeDtypeStruct((2, 128), f32)),
            in_specs=[anywhere, anywhere, anywhere],
            out_specs=(vmem, vmem, vmem),
            scratch_shapes=[
                pltpu.VMEM((CHUNKS, chunk, block), bf16),
                pltpu.VMEM((traits, block), f32),
                pltpu.VMEM((n_samp, 2, block), f32),
                pltpu.VMEM((4, 8, 128), f32),
                pltpu.VMEM((2, parts, CHUNKS, half, chunk + TAIL), jnp.int16),
                pltpu.VMEM((parts, CHUNKS, half, chunk), f32),
                pltpu.VMEM((2, parts, 6, CHUNKS, half, chunk + TAIL), jnp.int16),
                pltpu.VMEM((2, parts, half, block), f32),
                pltpu.VMEM((2, parts, half, block), f32),
                pltpu.VMEM((2, 2, parts, half, block), f32),
                pltpu.VMEM((line, 2, 128), f32),
                pltpu.VMEM((seats, 2, 128), f32),
                pltpu.SMEM((1,), jnp.int32),
                dma,
                dma((CHUNKS,)),
                dma,
                dma((n_samp - 1,)), dma((n_samp - 1,)),
                dma((3,)), dma((3,)),
                dma((2, parts, 6, CHUNKS)), dma((2, parts, 6, CHUNKS)),
                dma((2, 2, parts, 2)), dma((2, 2, parts, 2)),
                dma((line - 1,)), dma((line - 1,)),
                dma((seats - 1,)), dma((seats - 1,)),
            ],
            compiler_params=pltpu.CompilerParams(
                collective_id=0, has_side_effects=True,
                vmem_limit_bytes=GRANT,
            ),
        )(dosage, band_width, marginal.T)
        m0, m1, m2, mixed = (
            coefs[q // 2, q % 2 * traits : (q % 2 + 1) * traits] for q in range(4)
        )
        m3 = mixed - m2
        tau = penalty + 1.0
        mu1 = tau * m0 + m1
        alpha0 = m0 / mu1
        g = m1 / mu1
        rr1 = alpha0 * alpha0 * m2 - g * g * m0
        beta0 = rr1 / m0
        inner = g * g * m1 - 2.0 * g * alpha0 * m2 + alpha0 * alpha0 * m3
        curve = tau * rr1 + inner - beta0 * rr1 / alpha0
        alpha1 = rr1 / curve
        lead = g + beta0
        cross = alpha1 * alpha0
        b = marginal.T
        effects = (alpha0 + alpha1 * lead)[:, None] * b - cross[:, None] * p1
        residual = (
            (g - alpha1 * lead * tau)[:, None] * b
            + (cross * tau - alpha1 * lead - alpha0)[:, None] * p1
            + cross[:, None] * p2
        )
        return effects.T, residual.T

    in_specs = (P("samp", "snp"), P("snp"), P("snp", None), P())
    out_specs = (P("snp", None), P("snp", None))
    return jax.shard_map(step, mesh=mesh, in_specs=in_specs, out_specs=out_specs, check_vma=False)
```

time: 56.8 us -> 56.9 us (level)
  no operation moved by 1% of the time
where the time goes in v3:
time: 56.9 us; the launch traced here: 56.8 us
  Pallas kernels  54.4 us (96%)
  between operations  1.36 us (2%)
  other arithmetic  0.99 us (2%)
    pallas_call x1, Pallas kernels, step(): pl.pallas_call(functools.partial(kernel, n_samp, n_snp, line, mine * n_sa...  54.4 us

profile of v3, /device:TPU:1, one launch (start us, length us, event | category | flops | bytes accessed | tf_op | source)
XLA Modules:
  0.0 56.8 jit_solution(17891342359740725865)
XLA Ops:
  0.6 0.0 copy-start.1
  0.6 0.0 copy-start
  1.3 54.4 %shard_map.59 = (f32[64,512]{1,0:T(8,128)S(1)}, f32[64,512]{1,0:T(8,128)S(1)}, f32[2,128]{1,0:T(2,128)S(1)}) custom-call(bf16[2048,512]{1,0:T(8,128)(2,1)} %dosage.1, s32[1]{0:T(128)S(6)} %copy.6.width_hbm, f32[64,512]{1,0:T(8,128)} %bitcast.67), custom_call_target="tpu_custom_call" | custom-call | tf_op jit(solution)/shard_map/pallas_call | solution.py:375
  55.8 0.0 copy-done.1
  55.8 0.1 bitcast_divide_fusion.2
  55.9 0.1 multiply_subtract_fusion
  56.0 0.0 copy-done
  56.0 0.8 %add_bitcast_fusion = (f32[512,64]{0,1:T(8,128)}, f32[512,64]{0,1:T(8,128)}) fusion(f32[64,512]{1,0:T(8,128)S(1)} %get-tuple-element.7, f32[64,512]{1,0:T(8,128)S(1)} %get-tuple-element.6, f32[64]{0:T(128)S(1)} %get-tuple-element.11, f32[64]{0:T(128)S(1)} %get-tuple-element.8, f32[64]{0:T(128)S(1)} %get-tuple-element.12, f32[512,64]{0,1:T(8,128)S(1)} %copy-done, ...), kind=kLoop, calls=%fused_computation | loop fusion | flops 262144 | bytes 656384 | tf_op jit(solution)/shard_map/transpose | solution.py:431
  (1 shorter events, 0.0 us)
Async XLA Ops:
  0.6 55.2 %copy-start.1 = (f32[64]{0:T(128)S(1)}, f32[64]{0:T(128)}, u32[]{:S(2)}) copy-start(f32[64]{0:T(128)} %param.7) | copy-start | bytes 772
  0.6 55.3 %copy-start = (f32[512,64]{0,1:T(8,128)S(1)}, f32[512,64]{0,1:T(8,128)}, u32[]{:S(2)}) copy-start(f32[512,64]{0,1:T(8,128)} %param.6) | copy-start | bytes 393220

commit v4 on v3

--- a/solution.py
+++ b/solution.py
@@ -34,10 +34,10 @@
     n_samp, n_snp, line, samples,
     dosage, width_hbm, marginal,
     first_image, second_image, coefs,
-    grid, marg, stats, widths, own, own_f32, near, part, fold, fold_in,
+    grid, marg, stats, widths, own, own_f32, near, brief, brief_in, part, fold, fold_in,
     tile_a, tile_b, width, width_sem,
     load_sem, marg_sem, stat_send, stat_recv, width_send, width_recv,
-    u_send, u_recv, fold_send, fold_recv, a_send, a_recv, b_send, b_recv,
+    u_send, u_recv, brief_send, brief_recv, fold_send, fold_recv, a_send, a_recv, b_send, b_recv,
 ):
     chunk = grid.shape[1]
     block = grid.shape[2]
@@ -180,7 +180,7 @@
     flipped = (y + 1 - 2 * lax.rem(y, 2), i)
     mirrored = (n_samp - 1 - y, i)
     halves = range(traits // half)
-    moves, passed, legs = {}, {}, {}
+    moves, passed, legs, briefs = {}, {}, {}, {}
     cross = {}
 
     def hop(p, h, k, source, slot, peer):
@@ -205,14 +205,24 @@
         rows_out = vector.shape[0] // 2
         return u[:rows_out] + u[rows_out:]
 
+    def pack(target, values):
+        wide = values.shape[1]
+        peak = jnp.maximum(jnp.max(jnp.abs(values), 1, keepdims=True), 1e-30)
+        power = jnp.ceil(jnp.log2(peak * (1.0 / 32000.0)))
+        coded = jnp.round(values * jnp.exp2(-power))
+        target[:, 0:wide] = coded.astype(jnp.int32).astype(jnp.int16)
+        tail = jnp.broadcast_to(power, (values.shape[0], TAIL))
+        target[:, wide:] = tail.astype(jnp.int32).astype(jnp.int16)
+
+    def unpack(source, factor):
+        wide = source.shape[1] - TAIL
+        coded = source[:, 0:wide].astype(jnp.int32).astype(jnp.float32)
+        power = source[:, wide:].astype(jnp.int32).astype(jnp.float32)
+        return (factor * jnp.exp2(power[:, 0:1])) * coded
+
     def keep(p, h, k, u):
         own_f32[h, k] = u
-        peak = jnp.maximum(jnp.max(jnp.abs(u), 1, keepdims=True), 1e-30)
-        power = jnp.ceil(jnp.log2(peak * (1.0 / 32000.0)))
-        coded = jnp.round(u * jnp.exp2(-power))
-        own[p, h, k, :, 0:chunk] = coded.astype(jnp.int32).astype(jnp.int16)
-        tail = jnp.broadcast_to(power, (u.shape[0], TAIL))
-        own[p, h, k, :, chunk:] = tail.astype(jnp.int32).astype(jnp.int16)
+        pack(own.at[p, h, k], u)
 
     def forward(p, h):
         for k in range(CHUNKS):
@@ -231,9 +241,7 @@
         u = own_f32[h, k]
         w = u
         for slot, key in order:
-            coded = near[p, h, slot, k, :, 0:chunk].astype(jnp.int32).astype(jnp.float32)
-            power = near[p, h, slot, k, :, chunk:].astype(jnp.int32).astype(jnp.float32)
-            w = w + (masks[key] * jnp.exp2(power[:, 0:1])) * coded
+            w = w + unpack(near.at[p, h, slot, k], masks[key])
         if p == 1:
             piece = u * w
             folded = piece[:, 0:128]
@@ -256,6 +264,20 @@
             term = gather_back(w, k)
             total = term if total is None else total + term
         part[p, h] = (total[:half] + total[half:]) * (1.0 / samples)
+        if p == 1:
+            fold_start(p, h)
+            return
+        pack(brief.at[h], part[p, h])
+        briefs[h] = []
+        for d in range(1, n_samp):
+            copy = send(
+                brief.at[h], brief_in.at[h, d - 1],
+                brief_send.at[h, d - 1], brief_recv.at[h, d - 1], (samp_at(d), i),
+            )
+            copy.start()
+            briefs[h].append(copy)
+
+    def fold_start(p, h):
         legs[p, h, 0] = [fold_copy(p, h, 0, 0, flipped), fold_copy(p, h, 0, 1, mirrored)]
         for copy in legs[p, h, 0]:
             copy.start()
@@ -276,20 +298,25 @@
     def trait_cut(h):
         return pl.ds(h * half, half)
 
+    strip = min(256, chunk)
     for k in range(CHUNKS):
-        def standardize(r, carry, k=k):
-            cut = pl.ds(pl.multiple_of(r * rows, rows), rows)
+        for first_row in range(0, chunk, strip):
+            cut = pl.ds(first_row, strip)
             g = grid[k, cut, :].astype(jnp.float32)
-            grid[k, cut, :] = ((g - center) * scale).astype(jnp.bfloat16)
-            return carry
-
-        lax.fori_loop(0, chunk // rows, standardize, 0)
-        u = project(vector, k)
-        for h in halves:
-            keep(0, h, k, u[h * half : (h + 1) * half])
+            scaled = ((g - center) * scale).astype(jnp.bfloat16)
+            grid[k, cut, :] = scaled
+            u = lax.dot_general(
+                vector, scaled, (((1,), (1,)), ((), ())),
+                preferred_element_type=jnp.float32,
+            )
+            u = u[:traits] + u[traits:]
+            for h in halves:
+                own_f32[h, k, :, cut] = u[h * half : (h + 1) * half]
+        pack(own.at[0, 0, k], own_f32[0, k])
         send_own(0, 0, k)
     for h in halves[1:]:
         for k in range(CHUNKS):
+            pack(own.at[0, h, k], own_f32[h, k])
             send_own(0, h, k)
     make_masks()
     for h in halves:
@@ -297,17 +324,14 @@
     for h in halves:
         apply_band(0, h, lambda: None)
     for h in halves:
-        fold_once(0, h)
-
-    for h in halves:
-        image = fold_twice(0, h) - marg[trait_cut(h), :]
-        first_image[trait_cut(h), :] = image
-        vector = two_parts(image)
+        rough = part[0, h] - marg[trait_cut(h), :]
+        for d, copy in enumerate(briefs[h]):
+            copy.wait_recv()
+            rough = rough + unpack(brief_in.at[h, d], 1.0)
+        vector = two_parts(rough)
         for k in range(CHUNKS):
             keep(1, h, k, project(vector, k))
             send_own(1, h, k)
-    m1 = lanes_to_row(marg[...] * first_image[...])
-    m2 = lanes_to_row(first_image[...] * first_image[...])
     line_copies = []
 
     def send_sums():
@@ -323,7 +347,16 @@
             line_copies.append(copy)
 
     for h in halves:
+        fold_start(0, h)
+    for h in halves:
         forward(1, h)
+        if h == 0:
+            for other in halves:
+                fold_once(0, other)
+    for h in halves:
+        first_image[trait_cut(h), :] = fold_twice(0, h) - marg[trait_cut(h), :]
+    m1 = lanes_to_row(marg[...] * first_image[...])
+    m2 = lanes_to_row(first_image[...] * first_image[...])
     for h in halves:
         apply_band(1, h, send_sums if h == halves[-1] else lambda: None)
     for h in halves:
@@ -344,7 +377,7 @@
         plane_copies.append(copy)
     for h in halves:
         second_image[trait_cut(h), :] = fold_twice(1, h) - first_image[trait_cut(h), :]
-    for table in (moves, passed, legs):
+    for table in (moves, passed, legs, briefs):
         for group in table.values():
             started.extend(group)
     for copy in plane_copies:
@@ -385,6 +418,8 @@
                 pltpu.VMEM((2, parts, CHUNKS, half, chunk + TAIL), jnp.int16),
                 pltpu.VMEM((parts, CHUNKS, half, chunk), f32),
                 pltpu.VMEM((2, parts, 6, CHUNKS, half, chunk + TAIL), jnp.int16),
+                pltpu.VMEM((parts, half, block + TAIL), jnp.int16),
+                pltpu.VMEM((parts, n_samp - 1, half, block + TAIL), jnp.int16),
                 pltpu.VMEM((2, parts, half, block), f32),
                 pltpu.VMEM((2, parts, half, block), f32),
                 pltpu.VMEM((2, 2, parts, half, block), f32),
@@ -397,6 +432,7 @@
                 dma((n_samp - 1,)), dma((n_samp - 1,)),
                 dma((3,)), dma((3,)),
                 dma((2, parts, 6, CHUNKS)), dma((2, parts, 6, CHUNKS)),
+                dma((parts, n_samp - 1)), dma((parts, n_samp - 1)),
                 dma((2, 2, parts, 2)), dma((2, 2, parts, 2)),
                 dma((line - 1,)), dma((line - 1,)),
                 dma((seats - 1,)), dma((seats - 1,)),
@@ -412,12 +448,13 @@
         m3 = mixed - m2
         tau = penalty + 1.0
         mu1 = tau * m0 + m1
-        alpha0 = m0 / mu1
-        g = m1 / mu1
-        rr1 = alpha0 * alpha0 * m2 - g * g * m0
-        beta0 = rr1 / m0
+        inverse = 1.0 / mu1
+        alpha0 = m0 * inverse
+        g = m1 * inverse
+        beta0 = (m0 * m2 - m1 * m1) * inverse * inverse
+        rr1 = m0 * beta0
         inner = g * g * m1 - 2.0 * g * alpha0 * m2 + alpha0 * alpha0 * m3
-        curve = tau * rr1 + inner - beta0 * rr1 / alpha0
+        curve = tau * rr1 + inner - beta0 * beta0 * mu1
         alpha1 = rr1 / curve
         lead = g + beta0
         cross = alpha1 * alpha0

time: 56.9 us -> 55.9 us (0.982)
  Pallas kernels: 54.4 us -> 53.5 us
    pallas_call x1, Pallas kernels: 54.4 us -> 53.5 us  [step(): pl.pallas_call(functools.partial(kernel, n_samp, n_snp, line, mine * n_sa...]
where the time goes in v4:
time: 55.9 us; the launch traced here: 55.8 us
  Pallas kernels  53.5 us (96%)
  between operations  1.36 us (2%)
  other arithmetic  0.99 us (2%)
    pallas_call x1, Pallas kernels, step(): pl.pallas_call(functools.partial(kernel, n_samp, n_snp, line, mine * n_sa...  53.5 us

profile of v4, /device:TPU:1, one launch (start us, length us, event | category | flops | bytes accessed | tf_op | source)
XLA Modules:
  0.0 55.8 jit_solution(8376825970343554047)
XLA Ops:
  0.6 0.0 copy-start.1
  0.6 0.0 copy-start
  1.3 53.5 %shard_map.59 = (f32[64,512]{1,0:T(8,128)S(1)}, f32[64,512]{1,0:T(8,128)S(1)}, f32[2,128]{1,0:T(2,128)S(1)}) custom-call(bf16[2048,512]{1,0:T(8,128)(2,1)} %dosage.1, s32[1]{0:T(128)S(6)} %copy.6.width_hbm, f32[64,512]{1,0:T(8,128)} %bitcast.73), custom_call_target="tpu_custom_call" | custom-call | tf_op jit(solution)/shard_map/pallas_call | solution.py:408
  54.8 0.0 copy-done.1
  54.8 0.1 multiply_multiply_fusion
  54.9 0.1 multiply_subtract_fusion
  55.0 0.0 copy-done
  55.0 0.8 %add_bitcast_fusion = (f32[512,64]{0,1:T(8,128)}, f32[512,64]{0,1:T(8,128)}) fusion(f32[64,512]{1,0:T(8,128)S(1)} %get-tuple-element.7, f32[64,512]{1,0:T(8,128)S(1)} %get-tuple-element.6, f32[64]{0:T(128)S(1)} %get-tuple-element.12, f32[64]{0:T(128)S(1)} %get-tuple-element.8, f32[64]{0:T(128)S(1)} %get-tuple-element.13, f32[512,64]{0,1:T(8,128)S(1)} %copy-done, ...), kind=kLoop, calls=%fused_computation | loop fusion | flops 262144 | bytes 656384 | tf_op jit(solution)/shard_map/transpose | solution.py:468
  (1 shorter events, 0.0 us)
Async XLA Ops:
  0.6 54.2 %copy-start.1 = (f32[64]{0:T(128)S(1)}, f32[64]{0:T(128)}, u32[]{:S(2)}) copy-start(f32[64]{0:T(128)} %param.7) | copy-start | bytes 772
  0.6 54.3 %copy-start = (f32[512,64]{0,1:T(8,128)S(1)}, f32[512,64]{0,1:T(8,128)}, u32[]{:S(2)}) copy-start(f32[512,64]{0,1:T(8,128)} %param.6) | copy-start | bytes 393220

commit v5 on v4

--- a/solution.py
+++ b/solution.py
@@ -235,13 +235,15 @@
             passed[p, h, k] = [to_one, to_three, relay]
 
     def banded(p, h, k):
-        moves[p, h, k][2].wait_recv()
-        for copy in passed[p, h, k]:
-            copy.wait_recv()
+        to_one, to_three, relay = passed[p, h, k]
+        arrivals = {0: moves[p, h, k][2], 3: to_one, 2: to_three, 5: relay}
         u = own_f32[h, k]
         w = u
-        for slot, key in order:
-            w = w + unpack(near.at[p, h, slot, k], masks[key])
+        keys = dict(order)
+        for slot in (0, 1, 4, 3, 2, 5):
+            if slot in arrivals:
+                arrivals[slot].wait_recv()
+            w = w + unpack(near.at[p, h, slot, k], masks[keys[slot]])
         if p == 1:
             piece = u * w
             folded = piece[:, 0:128]

time: 55.9 us -> 55.5 us (level)
  no operation moved by 1% of the time
where the time goes in v5:
time: 55.5 us; the launch traced here: 55.4 us
  Pallas kernels  53 us (95%)
  between operations  1.36 us (2%)
  other arithmetic  0.99 us (2%)
    pallas_call x1, Pallas kernels, step(): pl.pallas_call(functools.partial(kernel, n_samp, n_snp, line, mine * n_sa...  53 us

profile of v5, /device:TPU:1, one launch (start us, length us, event | category | flops | bytes accessed | tf_op | source)
XLA Modules:
  0.0 55.4 jit_solution(170426881167800192)
XLA Ops:
  0.6 0.0 copy-start.1
  0.6 0.0 copy-start
  1.3 53.0 %shard_map.59 = (f32[64,512]{1,0:T(8,128)S(1)}, f32[64,512]{1,0:T(8,128)S(1)}, f32[2,128]{1,0:T(2,128)S(1)}) custom-call(bf16[2048,512]{1,0:T(8,128)(2,1)} %dosage.1, s32[1]{0:T(128)S(6)} %copy.6.width_hbm, f32[64,512]{1,0:T(8,128)} %bitcast.73), custom_call_target="tpu_custom_call" | custom-call | tf_op jit(solution)/shard_map/pallas_call | solution.py:410
  54.4 0.0 copy-done.1
  54.4 0.1 multiply_multiply_fusion
  54.5 0.1 multiply_subtract_fusion
  54.6 0.0 copy-done
  54.6 0.8 %add_bitcast_fusion = (f32[512,64]{0,1:T(8,128)}, f32[512,64]{0,1:T(8,128)}) fusion(f32[64,512]{1,0:T(8,128)S(1)} %get-tuple-element.7, f32[64,512]{1,0:T(8,128)S(1)} %get-tuple-element.6, f32[64]{0:T(128)S(1)} %get-tuple-element.12, f32[64]{0:T(128)S(1)} %get-tuple-element.8, f32[64]{0:T(128)S(1)} %get-tuple-element.13, f32[512,64]{0,1:T(8,128)S(1)} %copy-done, ...), kind=kLoop, calls=%fused_computation | loop fusion | flops 262144 | bytes 656384 | tf_op jit(solution)/shard_map/transpose | solution.py:470
  (1 shorter events, 0.0 us)
Async XLA Ops:
  0.6 53.7 %copy-start.1 = (f32[64]{0:T(128)S(1)}, f32[64]{0:T(128)}, u32[]{:S(2)}) copy-start(f32[64]{0:T(128)} %param.7) | copy-start | bytes 772
  0.6 53.9 %copy-start = (f32[512,64]{0,1:T(8,128)S(1)}, f32[512,64]{0,1:T(8,128)}, u32[]{:S(2)}) copy-start(f32[512,64]{0,1:T(8,128)} %param.6) | copy-start | bytes 393220
